TPU v7x, 32 devices: a whole 2x2x4 slice. The times are simulated.
32 devices in a mesh: pole: 2 (over y), col: 4 (over z), row: 4 (over x, core).
Axes of the slice: x: 2, y: 2, z: 4, core: 2. Of those that a mesh axis runs over, the one named last changes fastest.
Arguments:
- ancestor_inverse: bfloat16 [4, 2048, 2048], P('pole', 'col', 'row'), parts along dimension 0, may hold values from -0.125 to 0.125
- panels: bfloat16 [6, 2048, 512], P('pole', 'col'), parts along dimension 0, may hold values from -0.8984375 to 0.8984375
- block_lists: int32 [6, 16], P('pole'), parts along dimension 0, may hold values from -1 to 15, as said below
- diag_inverse: float32 [6, 256, 512], P('pole', ('col', 'row')), parts along dimension 0, may hold values from -6 to 6
Outputs:
- offdiag: bfloat16 [6, 2048, 512], P('pole', ('col', 'row')), parts along dimension 0
- diag_block: float32 [6, 256, 512], P('pole', ('col', 'row')), parts along dimension 0
There are 2 independent parts, one for each index of `pole`. A program takes and returns all parts, laid end to end along the dimension named above; each array names one. Nothing has to cross between parts.
Inputs may be any that keep to these rules, and one draw needn't show every extreme that they name: `block_lists`: in every supernode, the slots of range r hold distinct blocks of r * 4 to r * 4 + 3, filled slots first and -1 after them; every range has at least one filled slot, and some range has all 4 filled.
All inputs are finite; a program needn't handle non-finite values.
Results may differ from a plain program's by a relative error of at most 0.017.
Values may be sent and summed in bfloat16 or wider, within the bound.
No kernel may reach another device: no remote copies, remote signals or barrier semaphores. Data moves between devices by JAX's collectives and lax.ppermute only.
A program may use at most 64 MiB of HBM per device.

v0:
```python
import jax
import jax.numpy as jnp
from jax import lax
from jax.sharding import PartitionSpec as P

BS = 128
BPR = 4
CAP = 4


def from_root(value, axis, source):
    kept = jnp.where(lax.axis_index(axis) == source, value, 0).astype(value.dtype)
    return lax.psum(kept, axis)


def complex_product(first, second):
    half = first.shape[1] // 2
    return jnp.concatenate(
        [first[:, :half] - second[:, half:], first[:, half:] + second[:, :half]], axis=1
    )


def on_device(ancestor_inverse, panels, block_lists, diag_inverse):
    here_col = lax.axis_index("col")
    here_row = lax.axis_index("row")
    nsup = panels.shape[0]
    width = panels.shape[2] // 2
    mine = lax.dynamic_slice_in_dim(block_lists, here_col * CAP, CAP, 1)
    theirs = lax.dynamic_slice_in_dim(block_lists, here_row * CAP, CAP, 1)
    row_mask = jnp.repeat((mine >= 0).astype(jnp.bfloat16), BS, axis=1)
    masked = panels * row_mask[:, :, None]
    blocks = ancestor_inverse.reshape(2, BPR, BS, BPR, BS)
    pieces = []
    for k in range(nsup):
        range_rows = from_root(masked[k], "col", here_row)
        row_offset = jnp.clip(mine[k] - here_col * BPR, 0, BPR - 1)
        col_offset = jnp.clip(theirs[k] - here_row * BPR, 0, BPR - 1)
        picked = jnp.take(blocks, row_offset, axis=1)
        picked = jnp.take(picked, col_offset, axis=3).reshape(2, CAP * BS, CAP * BS)
        product_first = jnp.dot(picked[0], range_rows, preferred_element_type=jnp.float32)
        product_second = jnp.dot(picked[1], range_rows, preferred_element_type=jnp.float32)
        pieces.append(
            lax.psum_scatter(
                (
                    complex_product(product_first, product_second)
                    * row_mask[k][:, None].astype(jnp.float32)
                ).astype(jnp.bfloat16),
                "row",
                scatter_dimension=0,
                tiled=True,
            ).astype(jnp.float32)
        )
    summed = jnp.stack(pieces)
    offdiag = (-summed).astype(jnp.bfloat16)
    share = summed.shape[1]
    own_rows = lax.dynamic_slice_in_dim(masked, here_row * share, share, 1)
    dims = (((0,), (0,)), ((), ()))
    updates = []
    for k in range(nsup):
        first = lax.dot_general(
            own_rows[k][:, :width], offdiag[k], dims, preferred_element_type=jnp.float32
        )
        second = lax.dot_general(
            own_rows[k][:, width:], offdiag[k], dims, preferred_element_type=jnp.float32
        )
        updates.append(complex_product(first, second))
    updates = jnp.stack(updates)
    own_update = lax.psum_scatter(updates, ("col", "row"), scatter_dimension=1, tiled=True)
    return (offdiag, diag_inverse - own_update)


def solution(mesh):
    return jax.shard_map(
        on_device,
        mesh=mesh,
        in_specs=(
            P("pole", "col", "row"),
            P("pole", "col", None),
            P("pole", None),
            P("pole", ("col", "row"), None),
        ),
        out_specs=(P("pole", ("col", "row"), None), P("pole", ("col", "row"), None)),
        check_vma=False,
    )
```

profile of v0, /device:TPU:0, one launch (start us, length us, event | category | flops | bytes accessed | tf_op | source)
XLA Modules:
  0.0 227.8 jit_solution(14445422382365033342)
XLA Ops:
  7.2 0.8 compare_convert_fusion
  8.1 1.7 broadcast_multiply_fusion
  9.7 1.2 fusion.23
  11.0 0.6 copy-done.9
  11.8 0.4 copy-done.7
  12.2 1.1 reshape.115
  13.3 1.5 copy.31
  14.8 1.7 gather_fusion.4
  16.5 1.4 select_bitcast_fusion.1
  17.9 1.1 copy.40
  19.0 2.9 %gather_fusion.5 = bf16[4,2,4,128,128]{4,3,2,1,0:T(8,128)(2,1)} fusion(bf16[2,4,128,4,128]{4,2,3,1,0:T(8,128)(2,1)} %copy.40, s32[1024]{0:T(1024)S(1)} %pad_clamp_fusion), kind=kCustom, calls=%fused_computation.5.clone | custom fusion | bytes 2097168 | tf_op jit(solution)/shard_map/jit(_take)/gather | solution.py:39
  21.9 1.4 select_bitcast_fusion
  23.4 1.2 copy.41
  24.6 1.2 copy.42
  25.8 1.7 gather_fusion.2
  27.5 1.6 gather_fusion
  29.1 1.4 select_bitcast_fusion.3
  30.5 1.1 copy.36
  31.6 0.5 copy-done
  32.3 1.0 copy.32
  33.3 2.0 gather_fusion.1
  35.5 0.9 fusion.36
  36.3 0.4 copy.33
  36.8 2.0 gather_fusion.3
  39.0 1.2 copy.37
  40.3 1.2 copy.38
  41.5 0.4 copy.34
  42.0 40.9 %all-reduce.3.cloned.1.call-done = (bf16[512,512]{1,0:T(8,128)(2,1)}, bf16[512,512]{1,0:T(8,128)(2,1)}, bf16[512,512]{1,0:T(8,128)(2,1)}) async-done(((bf16[512,512]{1,0:T(8,128)(2,1)}, bf16[512,512]{1,0:T(8,128)(2,1)}, bf16[512,512]{1,0:T(8,128)(2,1)}), (bf16[512,512]{1,0:T(8,128)(2,1)}, bf16[512,512]{1,0:T(8,128)(2,1)}, bf16[512,512]{1,0:T(8,128)(2,1)})) %all-reduce.3.cloned.1.call-update) | async-done | bytes 1572880 | tf_op jit(solution)/shard_map/psum | solution.py:13
  82.9 1.7 fusion.3
  84.7 0.5 fusion.6
  85.5 1.0 copy.48
  86.6 1.8 fusion.9
  88.4 0.5 fusion.12
  89.2 1.0 copy.46
  90.3 1.6 fusion.15
  92.0 0.5 fusion.18
  92.8 1.0 copy.44
  94.0 13.5 %reduce-scatter.17.cloned.1.call-done = bf16[128,512]{1,0:T(8,128)(2,1)} async-done(((bf16[512,512]{1,0:T(8,128)(2,1)}), bf16[128,512]{1,0:T(8,128)(2,1)}) %reduce-scatter.17.cloned.1.call-update) | async-done | bytes 131088
  107.5 1.0 copy.49
  108.5 23.2 %reduce-scatter.15.cloned.1.call-done = bf16[128,512]{1,0:T(8,128)(2,1)} async-done(((bf16[512,512]{1,0:T(8,128)(2,1)}), bf16[128,512]{1,0:T(8,128)(2,1)}) %reduce-scatter.15.cloned.1.call-update) | async-done | bytes 131088
  131.7 1.0 copy.47
  132.7 23.0 %reduce-scatter.13.cloned.1.call-done = bf16[128,512]{1,0:T(8,128)(2,1)} async-done(((bf16[512,512]{1,0:T(8,128)(2,1)}), bf16[128,512]{1,0:T(8,128)(2,1)}) %reduce-scatter.13.cloned.1.call-update) | async-done | bytes 131088
  155.7 1.0 copy.45
  157.3 0.2 fusion.26
  158.7 1.3 pad_maximum_fusion
  160.1 0.9 copy.43
  161.0 58.7 %reduce-scatter.11.cloned.1.call-done = f32[3,16,512]{2,1,0:T(8,128)} async-done(((f32[3,256,512]{2,1,0:T(8,128)}), f32[3,16,512]{2,1,0:T(8,128)}) %reduce-scatter.11.cloned.1.call-update) | async-done | bytes 98320 | tf_op jit(solution)/shard_map/reduce_scatter | solution.py:68
  219.7 1.5 sub.69
  (64 shorter events, 4.1 us)
Async XLA Ops:
  7.2 75.8 %all-reduce.3.cloned.1.call-start = ((), (), s32[]{:S(2)}) async-start(), calls=%async_computation.8 | async-start | bytes 3145728 | tf_op jit(solution)/shard_map/psum | solution.py:13
  10.9 0.7 copy-start.9
  11.0 1.2 copy-start.7
  11.0 96.5 %reduce-scatter.17.cloned.1.call-start = ((), (), s32[]{:S(2)}) async-start(), calls=%async_computation.7 | async-start | bytes 655360
  30.5 1.6 copy-start
  39.0 2.4 %copy-start.3 = (bf16[1,4,128,4,128]{4,2,1,0,3:T(8,128)(2,1)S(1)}, bf16[1,4,128,4,128]{4,2,1,0,3:T(8,128)(2,1)}, u32[]{:S(2)}) copy-start(bf16[1,4,128,4,128]{4,2,1,0,3:T(8,128)(2,1)} %get-tuple-element.50) | copy-start | bytes 1572868
  41.5 43.2 %copy-start.1 = (bf16[1,4,128,4,128]{4,3,2,1,0:T(4,128)(2,1)S(1)}, bf16[1,4,128,4,128]{4,3,2,1,0:T(4,128)(2,1)}, u32[]{:S(2)}) copy-start(bf16[1,4,128,4,128]{4,3,2,1,0:T(4,128)(2,1)} %copy.41) | copy-start | bytes 1572868
  82.9 1.8 copy-start.6
  86.5 1.9 copy-start.2
  86.6 45.1 %reduce-scatter.15.cloned.1.call-start = ((), (), s32[]{:S(2)}) async-start(), calls=%async_computation.6 | async-start | bytes 655360
  86.6 1.8 copy-start.5
  90.3 1.7 copy-start.4
  90.3 65.4 %reduce-scatter.13.cloned.1.call-start = ((), (), s32[]{:S(2)}) async-start(), calls=%async_computation.5 | async-start | bytes 655360
  93.9 125.8 %reduce-scatter.11.cloned.1.call-start = ((), (), s32[]{:S(2)}) async-start(), calls=%async_computation.4 | async-start | bytes 1671168 | tf_op jit(solution)/shard_map/reduce_scatter | solution.py:68
  160.1 59.6 %copy-start.8 = (f32[3,16,512]{2,1,0:T(8,128)S(1)}, f32[3,16,512]{2,1,0:T(8,128)}, u32[]{:S(2)}) copy-start(f32[3,16,512]{2,1,0:T(8,128)} %param.11) | copy-start | bytes 294916
Sparse Core Ops, SparseCore 0:
  11.1 71.7 all-reduce.2
  86.7 20.7 reduce-scatter.16
  110.0 21.6 reduce-scatter.14
  134.0 21.6 reduce-scatter.12
  160.2 59.4 reduce-scatter.10
where the time goes:
time: 228 us
  waiting for transfers between devices  159 us (70%)
  local copies, waits for them, and re-layouts  33.3 us (15%)
  between operations  14.2 us (6%)
  other arithmetic  12.7 us (6%)
  matrix products  8.05 us (4%)
    unnamed x8, waiting for transfers between devices  59.8 us
    reduce_scatter x1, waiting for transfers between devices, on_device(): lax.psum_scatter(updates, ('col', 'row'), scatter_dimension=1, tiled=True)  58.7 us
    psum x1, waiting for transfers between devices, from_root(): return lax.psum(kept, axis)  40.9 us
    unnamed x29, local copies, waits for them, and re-layouts  8.66 us
    gather x3, local copies, waits for them, and re-layouts, on_device(): picked = jnp.take(picked, col_offset, axis=3).reshape(2, CAP * BS, CAP * BS)  6.85 us
    dot_general x3, matrix products, on_device(): jnp.dot(picked[1], range_rows, preferred_element_type=jnp.float32)  5.12 us
    gather x3, local copies, waits for them, and re-layouts, on_device(): picked = jnp.take(blocks, row_offset, axis=1)  5.01 us
  transfers between devices with their start and end apart: 5, of which 5 were waited for; matrix products, arithmetic and copies ran while one was open for 17% of the time, Pallas kernels for 0%

commit v1 on v0

--- a/solution.py
+++ b/solution.py
@@ -10,7 +10,7 @@
 
 def from_root(value, axis, source):
     kept = jnp.where(lax.axis_index(axis) == source, value, 0).astype(value.dtype)
-    return lax.psum(kept, axis)
+    return jnp.sum(lax.all_gather(kept, axis), axis=0)
 
 
 def complex_product(first, second):

time: 228 us -> 296 us (1.30)
  waiting for transfers between devices: 159 us -> 218 us
  other arithmetic: 12.7 us -> 22.8 us
    all_gather x0 -> x3, waiting for transfers between devices: none -> 94.1 us  [from_root(): return jnp.sum(lax.all_gather(kept, axis), axis=0)]
    psum x1 -> x0, waiting for transfers between devices: 40.9 us -> none  [from_root(): return lax.psum(kept, axis)]
    reduce_sum x0 -> x3, other arithmetic: none -> 6.53 us  [from_root(): return jnp.sum(lax.all_gather(kept, axis), axis=0)]
    unnamed x8 -> x10, waiting for transfers between devices: 59.8 us -> 65.6 us
    unnamed x29 -> x21, local copies, waits for them, and re-layouts: 8.66 us -> 7.27 us
  transfers between devices with their start and end apart: 5 -> 7, of which waited for: 5 -> 7; matrix products, arithmetic and copies ran while one was open for 17% -> 18% of each run, Pallas kernels for 0% -> 0%
where the time goes in v1:
time: 296 us; the launch traced here: 295 us
  waiting for transfers between devices  218 us (74%)
  local copies, waits for them, and re-layouts  32.3 us (11%)
  other arithmetic  22.8 us (8%)
  between operations  14.5 us (5%)
  matrix products  6.58 us (2%)
    all_gather x3, waiting for transfers between devices, from_root(): return jnp.sum(lax.all_gather(kept, axis), axis=0)  94.1 us
    unnamed x10, waiting for transfers between devices  65.6 us
    reduce_scatter x1, waiting for transfers between devices, on_device(): lax.psum_scatter(updates, ('col', 'row'), scatter_dimension=1, tiled=True)  58.7 us
    gather x3, local copies, waits for them, and re-layouts, on_device(): picked = jnp.take(picked, col_offset, axis=3).reshape(2, CAP * BS, CAP * BS)  7.91 us
    unnamed x21, local copies, waits for them, and re-layouts  7.27 us
    reduce_sum x3, other arithmetic, from_root(): return jnp.sum(lax.all_gather(kept, axis), axis=0)  6.53 us
  transfers between devices with their start and end apart: 7, of which 7 were waited for; matrix products, arithmetic and copies ran while one was open for 18% of the time, Pallas kernels for 0%

profile of v1, /device:TPU:0, one launch (start us, length us, event | category | flops | bytes accessed | tf_op | source)
XLA Modules:
  0.0 295.0 jit_solution(6540092812411950276)
XLA Ops:
  7.2 0.8 compare_convert_fusion
  8.1 1.7 broadcast_multiply_fusion
  9.7 1.2 slice_select_fusion.2
  11.0 0.7 all-gather.6.cloned.1.call-update
  11.8 0.7 all-gather.4.cloned.1.call-update
  12.5 1.1 reshape.106
  13.6 1.5 copy.31
  15.3 1.7 gather_fusion.4
  16.9 1.4 select_bitcast_fusion.1
  18.3 1.1 copy.40
  19.4 1.7 gather_fusion.2
  21.1 1.4 select_bitcast_fusion.3
  22.5 1.1 copy.36
  23.6 3.0 %gather_fusion.5 = bf16[4,2,4,128,128]{4,3,2,1,0:T(8,128)(2,1)} fusion(bf16[2,4,128,4,128]{4,2,3,1,0:T(8,128)(2,1)} %copy.40, s32[1024]{0:T(1024)S(1)} %pad_clamp_fusion), kind=kCustom, calls=%fused_computation.5.clone | custom fusion | bytes 2097168 | tf_op jit(solution)/shard_map/jit(_take)/gather | solution.py:39
  26.6 2.5 select_bitcast_fusion
  29.0 3.0 %gather_fusion.3 = bf16[4,2,4,128,128]{4,3,2,1,0:T(8,128)(2,1)} fusion(bf16[2,4,128,4,128]{4,2,3,1,0:T(8,128)(2,1)} %copy.36, s32[1024]{0:T(1024)S(1)} %pad_clamp_fusion.2), kind=kCustom, calls=%fused_computation.4.clone | custom fusion | bytes 2097168 | tf_op jit(solution)/shard_map/jit(_take)/gather | solution.py:39
  32.0 1.5 select_bitcast_fusion.2
  33.7 1.3 copy.42
  34.9 1.2 copy.41
  36.3 1.2 copy.38
  37.5 1.2 copy.37
  38.7 1.7 gather_fusion
  40.4 1.4 select_bitcast_fusion.5
  41.8 1.1 copy.32
  42.8 2.0 gather_fusion.1
  46.1 13.4 %all-gather.8.cloned.1.call-done = bf16[4,512,512]{2,1,0:T(8,128)(2,1)} async-done(((bf16[1,512,512]{2,1,0:T(8,128)(2,1)}), bf16[4,512,512]{2,1,0:T(8,128)(2,1)}) %all-gather.8.cloned.1.call-update) | async-done | bytes 2097168 | tf_op jit(solution)/shard_map/all_gather | solution.py:13
  59.5 2.2 reduce_sum.38
  61.7 1.6 fusion.3
  63.3 0.5 fusion.6
  64.1 1.1 copy.48
  65.3 40.3 %all-gather.6.cloned.1.call-done = bf16[4,512,512]{2,1,0:T(8,128)(2,1)} async-done(((bf16[1,512,512]{2,1,0:T(8,128)(2,1)}), bf16[4,512,512]{2,1,0:T(8,128)(2,1)}) %all-gather.6.cloned.1.call-update) | async-done | bytes 2097168 | tf_op jit(solution)/shard_map/all_gather | solution.py:13
  105.6 2.2 reduce_sum.37
  107.8 1.6 fusion.9
  109.4 0.5 fusion.12
  110.2 1.0 copy.46
  111.3 40.3 %all-gather.4.cloned.1.call-done = bf16[4,512,512]{2,1,0:T(8,128)(2,1)} async-done(((bf16[1,512,512]{2,1,0:T(8,128)(2,1)}), bf16[4,512,512]{2,1,0:T(8,128)(2,1)}) %all-gather.4.cloned.1.call-update) | async-done | bytes 2097168 | tf_op jit(solution)/shard_map/all_gather | solution.py:13
  151.6 2.2 reduce_sum.36
  155.1 1.0 copy.44
  156.3 18.2 %reduce-scatter.17.cloned.1.call-done = bf16[128,512]{1,0:T(8,128)(2,1)} async-done(((bf16[512,512]{1,0:T(8,128)(2,1)}), bf16[128,512]{1,0:T(8,128)(2,1)}) %reduce-scatter.17.cloned.1.call-update) | async-done | bytes 131088
  174.5 1.0 copy.49
  175.5 23.0 %reduce-scatter.15.cloned.1.call-done = bf16[128,512]{1,0:T(8,128)(2,1)} async-done(((bf16[512,512]{1,0:T(8,128)(2,1)}), bf16[128,512]{1,0:T(8,128)(2,1)}) %reduce-scatter.15.cloned.1.call-update) | async-done | bytes 131088
  198.5 1.0 copy.47
  199.5 23.0 %reduce-scatter.13.cloned.1.call-done = bf16[128,512]{1,0:T(8,128)(2,1)} async-done(((bf16[512,512]{1,0:T(8,128)(2,1)}), bf16[128,512]{1,0:T(8,128)(2,1)}) %reduce-scatter.13.cloned.1.call-update) | async-done | bytes 131088
  222.5 1.0 copy.45
  225.5 1.3 pad_maximum_fusion
  226.9 0.9 copy.43
  227.8 58.7 %reduce-scatter.11.cloned.1.call-done = f32[3,16,512]{2,1,0:T(8,128)} async-done(((f32[3,256,512]{2,1,0:T(8,128)}), f32[3,16,512]{2,1,0:T(8,128)}) %reduce-scatter.11.cloned.1.call-update) | async-done | bytes 98320 | tf_op jit(solution)/shard_map/reduce_scatter | solution.py:68
  286.6 1.5 sub.69
  (65 shorter events, 6.0 us)
Async XLA Ops:
  7.2 52.3 %all-gather.8.cloned.1.call-start = ((), (), s32[]{:S(2)}) async-start(), calls=%async_computation.6 | async-start | bytes 2621440 | tf_op jit(solution)/shard_map/all_gather | solution.py:13
  10.9 1.6 copy-start.3
  11.0 94.6 %all-gather.6.cloned.1.call-start = ((), (), s32[]{:S(2)}) async-start(), calls=%async_computation.5 | async-start | bytes 2621440 | tf_op jit(solution)/shard_map/all_gather | solution.py:13
  11.7 139.9 %all-gather.4.cloned.1.call-start = ((), (), s32[]{:S(2)}) async-start(), calls=%async_computation.4 | async-start | bytes 2621440 | tf_op jit(solution)/shard_map/all_gather | solution.py:13
  12.5 162.0 %reduce-scatter.17.cloned.1.call-start = ((), (), s32[]{:S(2)}) async-start(), calls=%async_computation.10 | async-start | bytes 655360
  13.6 1.5 copy-start.5
  32.0 1.6 copy-start
  61.7 1.6 copy-start.2
  65.2 133.3 %reduce-scatter.15.cloned.1.call-start = ((), (), s32[]{:S(2)}) async-start(), calls=%async_computation.9 | async-start | bytes 655360
  107.7 1.6 copy-start.1
  111.2 111.3 %reduce-scatter.13.cloned.1.call-start = ((), (), s32[]{:S(2)}) async-start(), calls=%async_computation.8 | async-start | bytes 655360
  156.2 130.4 %reduce-scatter.11.cloned.1.call-start = ((), (), s32[]{:S(2)}) async-start(), calls=%async_computation.7 | async-start | bytes 1671168 | tf_op jit(solution)/shard_map/reduce_scatter | solution.py:68
  226.9 59.7 %copy-start.4 = (f32[3,16,512]{2,1,0:T(8,128)S(1)}, f32[3,16,512]{2,1,0:T(8,128)}, u32[]{:S(2)}) copy-start(f32[3,16,512]{2,1,0:T(8,128)} %param.11) | copy-start | bytes 294916
Sparse Core Ops, SparseCore 0:
  11.1 48.3 all-gather.7
  61.1 44.4 all-gather.5
  107.1 44.4 all-gather.3
  154.0 20.4 reduce-scatter.16
  176.8 21.6 reduce-scatter.14
  200.8 21.6 reduce-scatter.12
  227.0 59.5 reduce-scatter.10
